TPU v7x, 512 devices: a whole 4x8x8 slice. The times are simulated.
512 devices in a mesh: dp: 4 (over x), expert: 32 (over z, y_lo), tensor: 4 (over y_hi, core).
Axes of the slice: x: 4, y: 8 (y_hi: 2, y_lo: 4; y = y_hi * 4 + y_lo), z: 8, core: 2. Of those that a mesh axis runs over, the one named last changes fastest.
Arguments:
- tokens: bfloat16 [16384, 7168], P(('dp', 'expert'), 'tensor'), may hold values from -6 to 6
- expert_ids: int32 [16384, 2], P(('dp', 'expert')), may hold values from 0 to 31, all different within a row; in each aligned block of 128 rows (0 to 127, 128 to 255, ...) at most 12 rows name the same one
- gate_scores: bfloat16 [16384, 2], P(('dp', 'expert')), may hold values from 0.099609375 to 0.59765625
- weight_in: bfloat16 [32, 2, 7168, 1024], P('expert', None, 'tensor', 'dp'), may hold values from -0.0625 to 0.0625
- weight_out: bfloat16 [32, 1024, 7168], P('expert', 'dp', 'tensor'), may hold values from -0.1875 to 0.1875
Outputs:
- mixed: bfloat16 [16384, 7168], P(('dp', 'expert'), 'tensor')
Inputs may be any that keep to these rules, and one draw needn't show every extreme that they name: `expert_ids`: each token names 2 different experts; among the 128 tokens of one index of dp and expert together (aligned blocks of rows) no expert is named more than 12 times, and in some blocks an expert is named exactly 12 times.
All inputs are finite; a program needn't handle non-finite values.
Results may differ from a plain program's by a relative error of at most 0.0071.
Values may be sent and summed in bfloat16 or wider, within the bound.
No kernel may reach another device: no remote copies, remote signals or barrier semaphores. Data moves between devices by JAX's collectives and lax.ppermute only.
A program may use at most 64 MiB of HBM per device.

v0:
```python
import jax
import jax.numpy as jnp
from jax import lax
from jax.sharding import Mesh
from jax.sharding import PartitionSpec as P

TENSOR = ("tensor_0", "tensor_1")


def one_axis_at_a_time(shard, axes):
    for axis in axes:
        shard = lax.psum(shard, axis)
    return shard


def in_blocks(shard, dim, devices):
    before, after = (shard.shape[:dim], shard.shape[dim + 1 :])
    return jnp.moveaxis(shard.reshape(*before, devices, -1, *after), dim, 0)


def sent_and_summed(shard, axis, dim):
    devices = lax.axis_size(axis)
    pieces = lax.all_to_all(in_blocks(shard, dim, devices), axis, 0, 0, tiled=True)
    return jnp.sum(pieces, axis=0)


def joined_along(pieces, dim):
    dims = list(pieces.shape[1:])
    dims[dim] *= pieces.shape[0]
    return jnp.moveaxis(pieces, 0, dim).reshape(dims)


def gather_in_order(shard, axes, order):
    pieces = shard[None]
    for k in order:
        pieces = lax.all_gather(pieces, axes[k], axis=0, tiled=True)
    held = [lax.axis_size(axes[k]) for k in reversed(order)]
    pieces = pieces.reshape(*held, *shard.shape)
    turned = sorted(range(len(order)), key=lambda place: order[len(order) - 1 - place])
    return pieces.transpose(*turned, *range(len(order), pieces.ndim)).reshape(-1, *shard.shape)


def gathered_by_axis(shard, axes, order, dim):
    return joined_along(gather_in_order(shard, axes, order), dim)


def per_device(tokens, expert_ids, gate_scores, weight_in, weight_out):
    experts = lax.axis_size("expert")
    tok_count, top_count = expert_ids.shape
    capacity = min(3 * tok_count * top_count // (2 * experts), tok_count)
    width_all = tokens.shape[1] * lax.axis_size(TENSOR)
    wide = tokens.astype(jnp.float32)
    row_squares = one_axis_at_a_time(jnp.sum(wide * wide, axis=1, keepdims=True), TENSOR)
    normed = (wide * lax.rsqrt(row_squares / width_all + 1e-06)).astype(jnp.bfloat16)
    flat_ids = expert_ids.reshape(-1)
    one_hot = (flat_ids[:, None] == jnp.arange(experts, dtype=jnp.int32)[None, :]).astype(jnp.int32)
    earlier = jnp.cumsum(one_hot, axis=0) - one_hot
    slot_pos = jnp.sum(earlier * one_hot, axis=1)
    target = flat_ids * capacity + slot_pos
    chosen = (target[:, None] == jnp.arange(experts * capacity, dtype=jnp.int32)[None, :]).astype(
        jnp.float32
    )
    chosen = chosen.reshape(tok_count, top_count, experts * capacity)
    picked = jnp.sum(chosen, axis=1).astype(jnp.bfloat16)
    combine_weight = jnp.sum(chosen * gate_scores.astype(jnp.float32)[:, :, None], axis=1).astype(
        jnp.bfloat16
    )
    outgoing = jnp.einsum("ts,td->sd", picked, normed, preferred_element_type=jnp.float32).astype(
        jnp.bfloat16
    )
    outgoing = outgoing.reshape(experts, capacity, tokens.shape[1])
    arrived = lax.all_to_all(outgoing, "expert", split_axis=0, concat_axis=0, tiled=True)
    slot_rows = arrived.reshape(experts * capacity, tokens.shape[1])
    local_in = weight_in[0]
    partial_sums = jnp.einsum(
        "rd,gdf->rgf",
        slot_rows,
        lax.all_gather(local_in, "dp", axis=2, tiled=True),
        preferred_element_type=jnp.float32,
    )
    summed = sent_and_summed(partial_sums, TENSOR, 2)
    hidden = (jax.nn.silu(summed[:, 0]) * summed[:, 1]).astype(jnp.bfloat16)
    hidden = hidden[:, None, :]
    row_count = hidden.shape[0]
    hidden_full = gathered_by_axis(hidden, TENSOR, (0, 1), 2).reshape(row_count, -1)
    expert_out = jnp.dot(
        hidden_full,
        lax.all_gather(weight_out[0], "dp", axis=0, tiled=True),
        preferred_element_type=jnp.float32,
    )
    sending = expert_out.astype(jnp.bfloat16).reshape(experts, capacity, weight_out.shape[2])
    returned = lax.all_to_all(sending, "expert", split_axis=0, concat_axis=0, tiled=True)
    mixed = jnp.dot(
        combine_weight,
        returned.reshape(experts * capacity, weight_out.shape[2]),
        preferred_element_type=jnp.float32,
    )
    return mixed.astype(jnp.bfloat16)


def solution(mesh):
    finer = Mesh(
        mesh.devices.reshape(mesh.shape["dp"], mesh.shape["expert"], 2, 2),
        ("dp", "expert", "tensor_0", "tensor_1"),
    )
    placed = (
        P(("dp", "expert"), TENSOR),
        P(("dp", "expert"), None),
        P(("dp", "expert"), None),
        P("expert", None, TENSOR, "dp"),
        P("expert", "dp", TENSOR),
    )
    return jax.shard_map(
        per_device,
        mesh=finer,
        in_specs=placed,
        out_specs=P(("dp", "expert"), TENSOR),
        check_vma=False,
    )
```

profile of v0, /device:TPU:16, one launch (start us, length us, event | category | flops | bytes accessed | tf_op | source)
XLA Modules:
  0.0 282.2 jit_solution(8761266857783817856)
XLA Ops:
  6.5 0.0 copy-start.1
  6.5 0.0 copy-start.2
  6.5 0.0 copy-start
  6.5 0.0 all-gather.5.cloned.1.call-start
  6.5 0.7 all-gather.5.cloned.1.call-update
  7.3 0.0 copy-done.1
  7.3 0.1 copy.47
  7.4 0.1 eq.39
  7.5 0.1 eq.43
  7.7 0.0 copy-done.2
  7.7 0.6 reduce-window.6
  8.3 0.2 slice_reduce_fusion
  8.5 0.1 fusion.16
  8.6 0.1 reduce_sum.48
  8.8 0.1 copy.50
  8.8 0.0 copy-done
  8.8 0.2 fusion.6
  9.0 8.8 %psum.14 = f32[128,1]{0,1:T(1,128)S(1)} all-reduce(f32[128,1]{0,1:T(1,128)S(1)} %bitcast.63), channel_id=1, replica_groups=mesh['dp'=4,'expert'=32,'tensor_0'=2,'tensor_1'=2] {'tensor_0'}, use_global_device_ids=true, to_apply=%region_6.7 | all-reduce | flops 128 | bytes 1024 | tf_op jit(solution)/shard_map/psum | solution.py:12
  17.9 2.4 psum.15
  20.3 0.1 select_reduce_fusion
  20.5 0.6 convolution_convert_fusion
  21.1 1.5 reshape.98
  22.6 13.8 %all-to-all-start = ((bf16[32,12,1792]{2,1,0:T(8,128)(2,1)}), bf16[32,12,1792]{2,1,0:T(8,128)(2,1)S(1)}, u32[]{:S(2)}, u32[]{:S(2)}) async-start(bf16[32,12,1792]{2,1,0:T(8,128)(2,1)} %reshape.98), calls=%async_computation | async-start | bytes 3670016 | tf_op jit(solution)/shard_map/all_to_all | solution.py:72
  36.4 0.0 all-gather.7.cloned.1.call-start
  36.5 0.7 all-gather.7.cloned.1.call-update
  37.2 43.4 %all-to-all-done = bf16[32,12,1792]{2,1,0:T(8,128)(2,1)S(1)} async-done(((bf16[32,12,1792]{2,1,0:T(8,128)(2,1)}), bf16[32,12,1792]{2,1,0:T(8,128)(2,1)S(1)}, u32[]{:S(2)}, u32[]{:S(2)}) %all-to-all-start) | async-done | bytes 1376288 | tf_op jit(solution)/shard_map/all_to_all | solution.py:72
  80.6 0.3 reshape.106
  80.9 16.9 %all-gather.5.cloned.1.call-done = bf16[1,2,1792,1024]{3,2,1,0:T(8,128)(2,1)} async-done(((bf16[1,2,1792,256]{3,2,1,0:T(8,128)(2,1)}), bf16[1,2,1792,1024]{3,2,1,0:T(8,128)(2,1)}) %all-gather.5.cloned.1.call-update) | async-done | bytes 7340048 | tf_op jit(solution)/shard_map/all_gather | solution.py:78
  97.9 10.1 %copy.51 = bf16[2,1024,1792]{2,1,0:T(8,128)(2,1)} copy(bf16[2,1024,1792]{1,2,0:T(8,128)(2,1)} %bitcast.58) | data formatting | bytes 14680064 | tf_op jit(solution)/shard_map/rd,gdf->rgf/dot_general | solution.py:75
  107.9 5.3 %convolution_bitcast_fusion = f32[4,384,2,256]{3,1,0,2:T(8,128)S(1)} fusion(bf16[2,4,256,1792]{3,2,1,0:T(8,128)(2,1)} %bitcast.59, bf16[384,1792,1,1]{1,0,2,3:T(8,128)(2,1)S(1)} %reshape.106), kind=kOutput, calls=%fused_computation.5 | convolution fusion | flops 2818572288 | bytes 11862016 | tf_op jit(solution)/shard_map/rd,gdf->rgf/dot_general | solution.py:75
  113.2 0.2 copy.52
  113.5 79.2 %all_to_all.15 = f32[4,384,2,256]{3,1,2,0:T(8,128)S(1)} all-to-all(f32[4,384,2,256]{3,1,2,0:T(8,128)S(1)} %copy.52), channel_id=1, replica_groups=mesh['dp'=4,'expert'=32,'tensor_0'=2,'tensor_1'=2] {'tensor_0','tensor_1'}, dimensions={0} | all-to-all | bytes 6291456 | tf_op jit(solution)/shard_map/all_to_all | solution.py:23
  192.7 1.2 reduce_sum.52
  193.8 1.2 fusion.11
  195.0 14.9 %all_gather.13 = bf16[2,384,1,256]{3,1,2,0:T(8,128)(2,1)S(1)} all-gather(bf16[1,384,1,256]{3,1,2,0:T(8,128)(2,1)S(1)} %fusion.11), channel_id=1, replica_groups=mesh['dp'=4,'expert'=32,'tensor_0'=2,'tensor_1'=2] {'tensor_0'}, dimensions={0}, use_global_device_ids=true | all-gather | bytes 589824 | tf_op jit(solution)/shard_map/all_gather | solution.py:36
  209.9 2.4 all_gather.14
  212.3 0.1 copy.53
  212.3 0.4 copy.54
  212.7 0.0 all-gather.7.cloned.1.call-done
  212.7 3.7 %fusion.2 = bf16[384,1792]{1,0:T(8,128)(2,1)S(1)} fusion(bf16[384,1024]{0,1:T(8,128)(2,1)S(1)} %bitcast.62, bf16[1,1024,1792]{2,1,0:T(8,128)(2,1)} %all-gather.7.cloned.1.call-done), kind=kOutput, calls=%fused_computation.3 | convolution fusion | flops 1409974272 | bytes 5832704 | tf_op jit(solution)/shard_map/dot_general | solution.py:86
  216.4 0.4 reshape.102
  216.8 55.0 %all_to_all.16 = bf16[32,12,1792]{2,1,0:T(8,128)(2,1)} all-to-all(bf16[32,12,1792]{2,1,0:T(8,128)(2,1)S(1)} %reshape.102), channel_id=1, replica_groups=mesh['dp'=4,'expert'=32,'tensor_0'=2,'tensor_1'=2] {'expert'}, dimensions={0} | all-to-all | bytes 2752512 | tf_op jit(solution)/shard_map/all_to_all | solution.py:92
  271.8 2.4 reshape.103
  274.1 1.2 convolution_convert_fusion.1
  (6 shorter events, 0.1 us)
Async XLA Ops:
  6.5 0.7 copy-start.1
  6.5 1.1 copy-start.2
  6.5 2.3 copy-start
  6.5 91.3 %all-gather.5.cloned.1.call-start = ((), (), s32[]{:S(2)}) async-start(), calls=%async_computation.3 | async-start | bytes 9175040 | tf_op jit(solution)/shard_map/all_gather | solution.py:78
  22.6 58.0 %all-to-all-start = ((bf16[32,12,1792]{2,1,0:T(8,128)(2,1)}), bf16[32,12,1792]{2,1,0:T(8,128)(2,1)S(1)}, u32[]{:S(2)}, u32[]{:S(2)}) async-start(bf16[32,12,1792]{2,1,0:T(8,128)(2,1)} %reshape.98), calls=%async_computation | async-start | bytes 3670016 | tf_op jit(solution)/shard_map/all_to_all | solution.py:72
  36.4 176.3 %all-gather.7.cloned.1.call-start = ((), (), s32[]{:S(2)}) async-start(), calls=%async_computation.4 | async-start | bytes 4587520 | tf_op jit(solution)/shard_map/all_gather | solution.py:88
Sparse Core Ops, SparseCore 0:
  9.5 88.3 all-gather.4
  100.0 49.7 all-gather.6
where the time goes:
time: 283 us; the launch traced here: 282 us
  blocking collectives  163 us (58%)
  waiting for transfers between devices  61.7 us (22%)
  local copies, waits for them, and re-layouts  16 us (6%)
  starting transfers between devices  13.9 us (5%)
  between operations  13.6 us (5%)
  matrix products  10.7 us (4%)
  other arithmetic  3.46 us (1%)
    all_to_all x1, blocking collectives, sent_and_summed(): lax.all_to_all(in_blocks(shard, dim, devices), axis, 0, 0, tiled=True)  79.2 us
    all_to_all x1, blocking collectives, per_device(): lax.all_to_all(sending, 'expert', split_axis=0, concat_axis=0, tiled=True)  55 us
    all_to_all x1, waiting for transfers between devices, per_device(): lax.all_to_all(outgoing, 'expert', split_axis=0, concat_axis=0, tiled=True)  43.4 us
    all_gather x2, blocking collectives, gather_in_order(): pieces = lax.all_gather(pieces, axes[k], axis=0, tiled=True)  17.2 us
    all_gather x1, waiting for transfers between devices, per_device(): lax.all_gather(local_in, 'dp', axis=2, tiled=True)  16.9 us
    all_to_all x1, starting transfers between devices, per_device(): lax.all_to_all(outgoing, 'expert', split_axis=0, concat_axis=0, tiled=True)  13.8 us
    psum x2, blocking collectives, one_axis_at_a_time(): shard = lax.psum(shard, axis)  11.3 us
    dot_general x1, local copies, waits for them, and re-layouts, per_device(): jnp.einsum('rd,gdf->rgf', slot_rows, lax.all_gather(local_in, 'dp', axis=...  10.1 us
  transfers between devices with their start and end apart: 3, of which 2 were waited for; matrix products, arithmetic and copies ran while one was open for 8% of the time, Pallas kernels for 0%

commit v1 on v0

--- a/solution.py
+++ b/solution.py
@@ -5,6 +5,11 @@
 from jax.sharding import PartitionSpec as P
 
 TENSOR = ("tensor_0", "tensor_1")
+
+
+def tiled_gather(x, axis, dim):
+    copies = jnp.concatenate([x] * lax.axis_size(axis), axis=dim)
+    return lax.all_to_all(copies, axis, dim, dim, tiled=True)
 
 
 def one_axis_at_a_time(shard, axes):
@@ -75,7 +80,7 @@
     partial_sums = jnp.einsum(
         "rd,gdf->rgf",
         slot_rows,
-        lax.all_gather(local_in, "dp", axis=2, tiled=True),
+        tiled_gather(local_in, "dp", 2),
         preferred_element_type=jnp.float32,
     )
     summed = sent_and_summed(partial_sums, TENSOR, 2)

time: 283 us -> 374 us (1.32)
  the two profiles are of different devices: /device:TPU:16 before, /device:TPU:18 now
where the time goes in v1:
time: 374 us; the launch traced here: 373 us
  blocking collectives  161 us (43%)
  waiting for transfers between devices  135 us (36%)
  starting transfers between devices  19.9 us (5%)
  other arithmetic  19 us (5%)
  local copies, waits for them, and re-layouts  16.2 us (4%)
  between operations  13.5 us (4%)
  matrix products  9.47 us (3%)
    all_to_all x1, waiting for transfers between devices, tiled_gather(): return lax.all_to_all(copies, axis, dim, dim, tiled=True)  109 us
    all_to_all x1, blocking collectives, per_device(): lax.all_to_all(sending, 'expert', split_axis=0, concat_axis=0, tiled=True)  65.6 us
    all_to_all x1, blocking collectives, sent_and_summed(): lax.all_to_all(in_blocks(shard, dim, devices), axis, 0, 0, tiled=True)  57.4 us
    all_gather x2, blocking collectives, gather_in_order(): pieces = lax.all_gather(pieces, axes[k], axis=0, tiled=True)  26.3 us
    all_to_all x1, waiting for transfers between devices, per_device(): lax.all_to_all(outgoing, 'expert', split_axis=0, concat_axis=0, tiled=True)  25.4 us
    all_to_all x1, starting transfers between devices, per_device(): lax.all_to_all(outgoing, 'expert', split_axis=0, concat_axis=0, tiled=True)  13.8 us
    concatenate x1, other arithmetic, tiled_gather(): copies = jnp.concatenate([x] * lax.axis_size(axis), axis=dim)  13.2 us
    psum x2, blocking collectives, one_axis_at_a_time(): shard = lax.psum(shard, axis)  11.3 us
  transfers between devices with their start and end apart: 3, of which 2 were waited for; matrix products, arithmetic and copies ran while one was open for 8% of the time, Pallas kernels for 0%

profile of v1, /device:TPU:18, one launch (start us, length us, event | category | flops | bytes accessed | tf_op | source)
XLA Modules:
  0.0 373.5 jit_solution(6425817786967752564)
XLA Ops:
  6.5 0.8 copy.49
  7.3 0.1 eq.39
  7.5 0.1 eq.43
  7.6 1.2 fusion.6
  8.8 8.8 %psum.14 = f32[128,1]{0,1:T(1,128)S(1)} all-reduce(f32[128,1]{0,1:T(1,128)S(1)} %bitcast.62), channel_id=1, replica_groups=mesh['dp'=4,'expert'=32,'tensor_0'=2,'tensor_1'=2] {'tensor_0'}, use_global_device_ids=true, to_apply=%region_6.7 | all-reduce | flops 128 | bytes 1024 | tf_op jit(solution)/shard_map/psum | solution.py:17
  17.6 2.4 psum.15
  20.1 0.7 convert_element_type.47
  20.8 0.6 reduce-window.6
  21.4 0.2 slice_reduce_fusion
  21.6 0.1 fusion.16
  21.7 0.1 reduce_sum.48
  21.8 0.1 copy.52
  21.9 0.7 multiply_add_fusion
  22.6 0.1 select_reduce_fusion
  22.7 1.6 convolution_convert_fusion
  24.4 1.5 reshape.98
  25.9 13.8 %all-to-all-start = ((bf16[32,12,1792]{2,1,0:T(8,128)(2,1)}), bf16[32,12,1792]{2,1,0:T(8,128)(2,1)S(1)}, u32[]{:S(2)}, u32[]{:S(2)}) async-start(bf16[32,12,1792]{2,1,0:T(8,128)(2,1)} %reshape.98), calls=%async_computation | async-start | bytes 3670016 | tf_op jit(solution)/shard_map/all_to_all | solution.py:77
  39.7 5.6 %copy.53 = bf16[1,2,1792,256]{2,1,3,0:T(2,128)(2,1)} copy(bf16[1,2,1792,256]{3,2,1,0:T(8,128)(2,1)} %param.8) | data formatting | bytes 3670016 | tf_op args[3]
  45.3 13.2 %pad_maximum_fusion = bf16[2,1792,1024]{1,0,2:T(2,128)(2,1)} fusion(bf16[2,1792,256]{1,0,2:T(2,128)(2,1)} %bitcast.58), kind=kLoop, calls=%fused_computation | loop fusion | flops 11010048 | bytes 9175040 | tf_op jit(solution)/shard_map/concatenate | solution.py:11
  58.5 25.4 %all-to-all-done = bf16[32,12,1792]{2,1,0:T(8,128)(2,1)S(1)} async-done(((bf16[32,12,1792]{2,1,0:T(8,128)(2,1)}), bf16[32,12,1792]{2,1,0:T(8,128)(2,1)S(1)}, u32[]{:S(2)}, u32[]{:S(2)}) %all-to-all-start) | async-done | bytes 1376288 | tf_op jit(solution)/shard_map/all_to_all | solution.py:77
  83.9 6.0 %all-to-all-start.1 = ((bf16[2,1792,1024]{1,0,2:T(2,128)(2,1)}), bf16[2,1792,1024]{1,0,2:T(2,128)(2,1)}, u32[]{:S(2)}, u32[]{:S(2)}) async-start(bf16[2,1792,1024]{1,0,2:T(2,128)(2,1)} %pad_maximum_fusion), calls=%async_computation.1 | async-start | bytes 14680064 | tf_op jit(solution)/shard_map/all_to_all | solution.py:12
  89.9 0.0 all-gather.3.cloned.1.call-start
  89.9 0.7 all-gather.3.cloned.1.call-update
  90.6 0.4 reshape.105
  91.0 108.6 %all-to-all-done.1 = bf16[2,1792,1024]{1,0,2:T(2,128)(2,1)} async-done(((bf16[2,1792,1024]{1,0,2:T(2,128)(2,1)}), bf16[2,1792,1024]{1,0,2:T(2,128)(2,1)}, u32[]{:S(2)}, u32[]{:S(2)}) %all-to-all-start.1) | async-done | bytes 7340064 | tf_op jit(solution)/shard_map/all_to_all | solution.py:12
  199.6 4.0 %copy.54 = bf16[2,1024,1792]{2,1,0:T(8,128)(2,1)S(1)} copy(bf16[2,1024,1792]{2,0,1:T(2,128)(2,1)} %bitcast.5) | data formatting | bytes 14680064 | tf_op jit(solution)/shard_map/rd,gdf->rgf/dot_general | solution.py:80
  203.6 3.0 convolution_bitcast_fusion
  206.6 0.2 copy.55
  206.8 57.4 %all_to_all.20 = f32[4,384,2,256]{3,1,2,0:T(8,128)S(1)} all-to-all(f32[4,384,2,256]{3,1,2,0:T(8,128)S(1)} %copy.55), channel_id=1, replica_groups=mesh['dp'=4,'expert'=32,'tensor_0'=2,'tensor_1'=2] {'tensor_0','tensor_1'}, dimensions={0} | all-to-all | bytes 6291456 | tf_op jit(solution)/shard_map/all_to_all | solution.py:28
  264.3 1.2 reduce_sum.52
  265.4 1.2 fusion.11
  266.7 24.0 %all_gather.9 = bf16[2,384,1,256]{3,1,2,0:T(8,128)(2,1)S(1)} all-gather(bf16[1,384,1,256]{3,1,2,0:T(8,128)(2,1)S(1)} %fusion.11), channel_id=1, replica_groups=mesh['dp'=4,'expert'=32,'tensor_0'=2,'tensor_1'=2] {'tensor_0'}, dimensions={0}, use_global_device_ids=true | all-gather | bytes 589824 | tf_op jit(solution)/shard_map/all_gather | solution.py:41
  290.6 2.4 all_gather.10
  293.0 0.1 copy.56
  293.1 0.4 copy.57
  293.4 0.0 all-gather.3.cloned.1.call-done
  293.4 3.7 fusion.2
  297.1 0.4 reshape.102
  297.5 65.6 %all_to_all.21 = bf16[32,12,1792]{2,1,0:T(8,128)(2,1)} all-to-all(bf16[32,12,1792]{2,1,0:T(8,128)(2,1)S(1)} %reshape.102), channel_id=1, replica_groups=mesh['dp'=4,'expert'=32,'tensor_0'=2,'tensor_1'=2] {'expert'}, dimensions={0} | all-to-all | bytes 2752512 | tf_op jit(solution)/shard_map/all_to_all | solution.py:97
  363.1 2.4 reshape.103
  365.5 1.2 convolution_convert_fusion.1
  (4 shorter events, 0.1 us)
Async XLA Ops:
  25.9 58.0 %all-to-all-start = ((bf16[32,12,1792]{2,1,0:T(8,128)(2,1)}), bf16[32,12,1792]{2,1,0:T(8,128)(2,1)S(1)}, u32[]{:S(2)}, u32[]{:S(2)}) async-start(bf16[32,12,1792]{2,1,0:T(8,128)(2,1)} %reshape.98), calls=%async_computation | async-start | bytes 3670016 | tf_op jit(solution)/shard_map/all_to_all | solution.py:77
  83.9 115.7 %all-to-all-start.1 = ((bf16[2,1792,1024]{1,0,2:T(2,128)(2,1)}), bf16[2,1792,1024]{1,0,2:T(2,128)(2,1)}, u32[]{:S(2)}, u32[]{:S(2)}) async-start(bf16[2,1792,1024]{1,0,2:T(2,128)(2,1)} %pad_maximum_fusion), calls=%async_computation.1 | async-start | bytes 14680064 | tf_op jit(solution)/shard_map/all_to_all | solution.py:12
  89.9 203.6 %all-gather.3.cloned.1.call-start = ((), (), s32[]{:S(2)}) async-start(), calls=%async_computation.4 | async-start | bytes 4587520 | tf_op jit(solution)/shard_map/all_gather | solution.py:93
Sparse Core Ops, SparseCore 0:
  92.8 77.7 all-gather.2
